TPU v7x, 512 devices: a whole 4x4x16 slice. The times are simulated.
512 devices in a mesh: dom: 128 (over z, y, core), src: 4 (over x).
Axes of the slice: x: 4, y: 4, z: 16, core: 2. Of those that a mesh axis runs over, the one named last changes fastest.
Arguments:
- features: bfloat16 [524288, 256], P(('dom', 'src')), may hold values from -6 to 6
- cotangent: bfloat16 [524288, 256], P(('dom', 'src')), may hold values from -6 to 6
- w_self: bfloat16 [256, 256], replicated, may hold values from -0.375 to 0.375
- w_neigh: bfloat16 [256, 256], replicated, may hold values from -0.375 to 0.375
- bias: bfloat16 [256], replicated, may hold values from -3 to 3
- send_rows: int32 [128, 4, 128, 8], P('dom', 'src'), may hold values from -1 to 1023, as said below
- edge_src: int32 [128, 4, 8192], P('dom', 'src'), may hold values from 0 to 2047, as said below
- edge_dst: int32 [128, 4, 8192], P('dom', 'src'), may hold values from 0 to 4095
- tile_count: int32 [128, 4], P('dom', 'src'), may hold values from 16 to 64, as said below
Outputs:
- activations: bfloat16 [524288, 256], P(('dom', 'src'))
- feature_grad: float32 [524288, 256], P(('dom', 'src'))
Inputs may be any that keep to these rules, and one draw needn't show every extreme that they name: `send_rows`: slots of a list are filled from the first one; some list of every owner is full; an account's own part sends it nothing. `edge_src`: every edge refers to a local row or to a filled slot. Edge slots after the first tile_count * 128 are ignored.
All inputs are finite; a program needn't handle non-finite values.
Results may differ from a plain program's by a relative error of at most 0.009.
Values may be sent and summed in bfloat16 or wider, within the bound.
No kernel may reach another device: no remote copies, remote signals or barrier semaphores. Data moves between devices by JAX's collectives and lax.ppermute only.
A program may use at most 64 MiB of HBM per device.

v0:
```python
import jax
import jax.numpy as jnp
from jax import lax
from jax.sharding import PartitionSpec as P


def local(features, cotangent, w_self, w_neigh, bias, send_rows, edge_src, edge_dst, tile_count):
    node_rows = features.shape[0]
    feature_width = features.shape[1]
    peer_total = lax.axis_size("dom")
    senders = send_rows[0, 0]
    capacity = senders.shape[1]
    halo_total = peer_total * capacity
    sources = edge_src[0, 0]
    targets = edge_dst[0, 0]
    edge_total = sources.shape[0]
    part_total = node_rows * lax.axis_size("src")
    active = jnp.arange(edge_total) // 128 < tile_count[0, 0]
    filled = senders >= 0
    zero_half = jnp.zeros((), jnp.bfloat16)
    picked = jnp.where(filled[:, :, None], features[jnp.maximum(senders, 0)], zero_half)
    counts = jnp.zeros((part_total,), jnp.float32).at[targets].add(active.astype(jnp.float32))
    degree_all = lax.psum(counts, "src")
    inverse_all = 1.0 / jnp.maximum(degree_all, 1.0)
    inverse = lax.dynamic_slice_in_dim(inverse_all, lax.axis_index("src") * node_rows, node_rows)
    remote = lax.all_to_all(picked, "dom", split_axis=0, concat_axis=0, tiled=True).reshape(
        halo_total, feature_width
    )
    table = jnp.concatenate([features, remote], axis=0)
    taken = jnp.where(active[:, None], table[sources], zero_half)
    partial_value = (
        jnp.zeros((part_total, feature_width), jnp.float32)
        .at[targets]
        .add(taken.astype(jnp.float32))
    )
    totals = lax.psum_scatter(
        partial_value.astype(jnp.bfloat16), "src", scatter_dimension=0, tiled=True
    ).astype(jnp.float32)
    neighbour_mean = (totals * inverse[:, None]).astype(jnp.bfloat16)
    preact = (
        jnp.dot(features, w_self, preferred_element_type=jnp.float32)
        + jnp.dot(neighbour_mean, w_neigh, preferred_element_type=jnp.float32)
        + bias.astype(jnp.float32)
    )
    sigma = jax.nn.sigmoid(preact)
    outputs = (preact * sigma).astype(jnp.bfloat16)
    slope = sigma * (1.0 + preact * (1.0 - sigma))
    upstream = (cotangent.astype(jnp.float32) * slope).astype(jnp.bfloat16)
    grad_own = jnp.dot(upstream, w_self.T, preferred_element_type=jnp.float32)
    scaled = (
        jnp.dot(upstream, w_neigh.T, preferred_element_type=jnp.float32) * inverse[:, None]
    ).astype(jnp.bfloat16)
    spread = lax.all_gather(scaled, "src", axis=0, tiled=True)
    contrib = jnp.where(active[:, None], spread[targets], zero_half).astype(jnp.float32)
    grad_table = (
        jnp.zeros((node_rows + halo_total, feature_width), jnp.float32).at[sources].add(contrib)
    )
    remote_grad = grad_table[node_rows:]
    local_grad = grad_table[:node_rows]
    returned = lax.all_to_all(
        remote_grad.reshape(peer_total, capacity, feature_width).astype(jnp.bfloat16),
        "dom",
        split_axis=0,
        concat_axis=0,
        tiled=True,
    ).astype(jnp.float32)
    back_rows = jnp.where(filled, senders, node_rows)
    incoming = (
        jnp.zeros((node_rows, feature_width), jnp.float32).at[back_rows].add(returned, mode="drop")
    )
    return (outputs, grad_own + local_grad + incoming)


def solution(mesh):
    placed = (
        P(("dom", "src"), None),
        P(("dom", "src"), None),
        P(),
        P(),
        P(),
        P("dom", "src", None, None),
        P("dom", "src", None),
        P("dom", "src", None),
        P("dom", "src"),
    )
    return jax.shard_map(
        local,
        mesh=mesh,
        in_specs=placed,
        out_specs=(P(("dom", "src"), None), P(("dom", "src"), None)),
        check_vma=False,
    )
```

profile of v0, /device:TPU:33, one launch (start us, length us, event | category | flops | bytes accessed | tf_op | source)
XLA Modules:
  0.0 406.9 jit_solution(14900899894254317384)
XLA Ops:
  7.2 0.8 compare_select_fusion.2
  8.0 0.7 compare_bitcast_fusion
  8.7 0.1 copy.13
  8.8 0.1 reshape.127
  8.9 0.1 copy.12
  9.0 4.6 %gather_fusion = bf16[1024,256]{1,0:T(8,128)(2,1)S(1)} fusion(bf16[1024,256]{1,0:T(8,128)(2,1)} %param.9, s32[1024]{0:T(1024)S(1)} %broadcast_clamp_fusion.2), kind=kCustom, calls=%fused_computation | custom fusion | bytes 1052672 | tf_op jit(solution)/shard_map/gather | solution.py:21
  13.6 1.0 bitcast_select_fusion
  14.6 19.5 %all-to-all-start = ((bf16[128,8,256]{2,1,0:T(8,128)(2,1)}), bf16[128,8,256]{2,1,0:T(8,128)(2,1)S(1)}, u32[]{:S(2)}, u32[]{:S(2)}) async-start(bf16[128,8,256]{2,1,0:T(8,128)(2,1)} %bitcast_select_fusion), calls=%async_computation | async-start | bytes 1048576 | tf_op jit(solution)/shard_map/all_to_all | solution.py:26
  34.9 32.7 %all-to-all-done = bf16[128,8,256]{2,1,0:T(8,128)(2,1)S(1)} async-done(((bf16[128,8,256]{2,1,0:T(8,128)(2,1)}), bf16[128,8,256]{2,1,0:T(8,128)(2,1)S(1)}, u32[]{:S(2)}, u32[]{:S(2)}) %all-to-all-start) | async-done | bytes 524320 | tf_op jit(solution)/shard_map/all_to_all | solution.py:26
  67.7 76.8 %scatter_custom_fusion = f32[4096,256]{1,0:T(8,128)} fusion(s32[8192]{0:T(1024)S(1)} %bitcast.39, pred[8192]{0:T(1024)(128)(4,1)S(1)} %fusion.19, bf16[]{:T(256)} %constant.41.clone.1, f32[]{:T(128)} %constant.14.clone.1, bf16[2048,256]{1,0:T(8,128)(2,1)S(1)} %pad_maximum_fusion, s32[8192]{0:T(1024)S(1)} %broadcast_clamp_fusion.1), kind=kCustom, calls=%fused_computation.9 | custom fusion | flops 6291456 | bytes 5283846 | tf_op jit(solution)/shard_map/scatter-add | solution.py:34
  144.6 3.8 convert_element_type.41
  148.4 43.2 %scatter_custom_fusion.1 = f32[4096]{0:T(1024)S(1)} fusion(s32[8192]{0:T(1024)S(1)} %bitcast.40, f32[8192]{0:T(1024)S(1)} %fusion.25, f32[]{:T(128)} %constant.14.clone.1), kind=kCustom, calls=%fused_computation.50 | custom fusion | flops 8192 | bytes 16388 | tf_op jit(solution)/shard_map/scatter-add | solution.py:22
  191.7 13.2 %psum.7 = f32[4096]{0:T(1024)S(1)} all-reduce(f32[4096]{0:T(1024)S(1)} %scatter_custom_fusion.1), channel_id=1, replica_groups=mesh['dom'=128,'src'=4] {'src'}, use_global_device_ids=true, to_apply=%region_3.4 | all-reduce | flops 4096 | bytes 32768 | tf_op jit(solution)/shard_map/psum | solution.py:23
  204.8 0.3 fusion.29
  205.2 2.6 multiply_convert_fusion
  207.8 1.1 fusion.12
  208.9 31.2 %all-gather.2.cloned.1.call-done = bf16[4096,256]{1,0:T(8,128)(2,1)} async-done(((bf16[1024,256]{1,0:T(8,128)(2,1)}), bf16[4096,256]{1,0:T(8,128)(2,1)}) %all-gather.2.cloned.1.call-update) | async-done | bytes 2097168 | tf_op jit(solution)/shard_map/all_gather | solution.py:53
  240.1 100.4 %scatter_custom_fusion.2 = f32[2048,256]{1,0:T(8,128)S(1)} fusion(s32[8192]{0:T(1024)S(1)} %bitcast.38, pred[8192]{0:T(1024)(128)(4,1)S(1)} %fusion.19, bf16[]{:T(256)} %constant.41.clone.1, f32[]{:T(128)} %constant.14.clone.1, bf16[4096,256]{1,0:T(8,128)(2,1)} %all-gather.2.cloned.1.call-done, s32[8192]{0:T(1024)S(1)} %broadcast_clamp_fusion), kind=kCustom, calls=%fused_computation.7 | custom fusion | flops 6291456 | bytes 4235270 | tf_op jit(solution)/shard_map/scatter-add | solution.py:56
  340.5 0.8 fusion.16
  341.4 16.8 %all-to-all-start.1 = ((bf16[128,8,256]{2,1,0:T(8,128)(2,1)}), bf16[128,8,256]{2,1,0:T(8,128)(2,1)S(1)}, u32[]{:S(2)}, u32[]{:S(2)}) async-start(bf16[128,8,256]{2,1,0:T(8,128)(2,1)} %fusion.16), calls=%async_computation.2 | async-start | bytes 1048576 | tf_op jit(solution)/shard_map/all_to_all | solution.py:60
  358.2 0.1 copy.14
  358.4 1.3 convolution_add_fusion
  359.7 32.1 %all-to-all-done.1 = bf16[128,8,256]{2,1,0:T(8,128)(2,1)S(1)} async-done(((bf16[128,8,256]{2,1,0:T(8,128)(2,1)}), bf16[128,8,256]{2,1,0:T(8,128)(2,1)S(1)}, u32[]{:S(2)}, u32[]{:S(2)}) %all-to-all-start.1) | async-done | bytes 524320 | tf_op jit(solution)/shard_map/all_to_all | solution.py:60
  391.8 8.3 %scatter_custom_fusion.3 = f32[1024,256]{1,0:T(8,128)} fusion(f32[1024,256]{1,0:T(8,128)} %convolution_add_fusion, s32[1024]{0:T(1024)S(1)} %reshape.175, bf16[128,8,256]{2,1,0:T(8,128)(2,1)S(1)} %all-to-all-done.1), kind=kCustom, calls=%fused_computation.25 | custom fusion | flops 524288 | bytes 1572864 | tf_op jit(solution)/shard_map/scatter-add | solution.py:69
  (30 shorter events, 0.5 us)
Async XLA Ops:
  7.2 198.0 %copy-start = (bf16[256,256]{1,0:T(8,128)(2,1)S(1)}, bf16[256,256]{1,0:T(8,128)(2,1)}, u32[]{:S(2)}) copy-start(bf16[256,256]{1,0:T(8,128)(2,1)} %param.12) | copy-start | bytes 393220
  7.2 60.5 %copy-start.1 = (bf16[1024,256]{1,0:T(8,128)(2,1)S(1)}, bf16[1024,256]{1,0:T(8,128)(2,1)}, u32[]{:S(2)}) copy-start(bf16[1024,256]{1,0:T(8,128)(2,1)} %param.9) | copy-start | bytes 1572868
  7.2 27.6 %copy-start.3 = (s32[1,1,8192]{2,1,0:T(1,128)S(1)}, s32[1,1,8192]{2,1,0:T(1,128)}, u32[]{:S(2)}) copy-start(s32[1,1,8192]{2,1,0:T(1,128)} %param.15) | copy-start | bytes 98308
  7.2 27.6 %copy-start.4 = (s32[1,1,8192]{2,1,0:T(1,128)S(1)}, s32[1,1,8192]{2,1,0:T(1,128)}, u32[]{:S(2)}) copy-start(s32[1,1,8192]{2,1,0:T(1,128)} %param.16) | copy-start | bytes 98308
  14.6 53.1 %all-to-all-start = ((bf16[128,8,256]{2,1,0:T(8,128)(2,1)}), bf16[128,8,256]{2,1,0:T(8,128)(2,1)S(1)}, u32[]{:S(2)}, u32[]{:S(2)}) async-start(bf16[128,8,256]{2,1,0:T(8,128)(2,1)} %bitcast_select_fusion), calls=%async_computation | async-start | bytes 1048576 | tf_op jit(solution)/shard_map/all_to_all | solution.py:26
  34.1 171.1 %reduce-scatter.2.cloned.1.call-start = ((), (), s32[]{:S(2)}) async-start(), calls=%async_computation.3 | async-start | bytes 2621440 | tf_op jit(solution)/shard_map/reduce_scatter | solution.py:36
  144.6 47.1 %copy-start.6 = (bf16[256]{0:T(256)(128)(2,1)S(1)}, bf16[256]{0:T(256)(128)(2,1)}, u32[]{:S(2)}) copy-start(bf16[256]{0:T(256)(128)(2,1)} %param.13) | copy-start | bytes 1540
  144.6 60.3 %copy-start.2 = (bf16[256,256]{1,0:T(8,128)(2,1)S(1)}, bf16[256,256]{1,0:T(8,128)(2,1)}, u32[]{:S(2)}) copy-start(bf16[256,256]{1,0:T(8,128)(2,1)} %param.11) | copy-start | bytes 393220
  144.6 60.6 %copy-start.5 = (bf16[1024,256]{1,0:T(8,128)(2,1)S(1)}, bf16[1024,256]{1,0:T(8,128)(2,1)}, u32[]{:S(2)}) copy-start(bf16[1024,256]{1,0:T(8,128)(2,1)} %param.10) | copy-start | bytes 1572868
  148.4 91.8 %all-gather.2.cloned.1.call-start = ((), (), s32[]{:S(2)}) async-start(), calls=%async_computation.4 | async-start | bytes 2621440 | tf_op jit(solution)/shard_map/all_gather | solution.py:53
  341.4 50.4 %all-to-all-start.1 = ((bf16[128,8,256]{2,1,0:T(8,128)(2,1)}), bf16[128,8,256]{2,1,0:T(8,128)(2,1)S(1)}, u32[]{:S(2)}, u32[]{:S(2)}) async-start(bf16[128,8,256]{2,1,0:T(8,128)(2,1)} %fusion.16), calls=%async_computation.2 | async-start | bytes 1048576 | tf_op jit(solution)/shard_map/all_to_all | solution.py:60
Sparse Core Ops, SparseCore 0:
  148.5 28.3 reduce-scatter.1
  209.0 31.0 all-gather.1
where the time goes:
time: 408 us; the launch traced here: 407 us
  other arithmetic  235 us (58%)
  waiting for transfers between devices  96.1 us (24%)
  starting transfers between devices  36.4 us (9%)
  between operations  14.9 us (4%)
  blocking collectives  13.2 us (3%)
  local copies, waits for them, and re-layouts  5.95 us (1%)
  matrix products  5.3 us (1%)
    scatter-add x1, other arithmetic, local(): jnp.zeros((node_rows + halo_total, feature_width), jnp.float32).at[sources]  100 us
    scatter-add x1, other arithmetic, local(): partial_value = jnp.zeros((part_total, feature_width), jnp.float32).at[ta...  76.8 us
    scatter-add x1, other arithmetic, local(): jnp.zeros((part_total,), jnp.float32).at[targets]  43.2 us
    all_to_all x1, waiting for transfers between devices, local(): lax.all_to_all(picked, 'dom', split_axis=0, concat_axis=0, tiled=True)  32.7 us
    all_to_all x1, waiting for transfers between devices, local(): lax.all_to_all(remote_grad.reshape(peer_total, capacity, feature_width).a...  32.1 us
    all_gather x1, waiting for transfers between devices, local(): spread = lax.all_gather(scaled, 'src', axis=0, tiled=True)  31.2 us
    all_to_all x1, starting transfers between devices, local(): lax.all_to_all(picked, 'dom', split_axis=0, concat_axis=0, tiled=True)  19.5 us
    all_to_all x1, starting transfers between devices, local(): lax.all_to_all(remote_grad.reshape(peer_total, capacity, feature_width).a...  16.8 us
  transfers between devices with their start and end apart: 4, of which 3 were waited for; matrix products, arithmetic and copies ran while one was open for 11% of the time, Pallas kernels for 0%

commit v1 on v0

--- a/solution.py
+++ b/solution.py
@@ -2,6 +2,27 @@
 import jax.numpy as jnp
 from jax import lax
 from jax.sharding import PartitionSpec as P
+
+
+def gather_around(x, axis, dim):
+    size, index, span = (lax.axis_size(axis), lax.axis_index(axis), x.shape[dim])
+    right = [(i, (i + 1) % size) for i in range(size)]
+    left = [(i, (i - 1) % size) for i in range(size)]
+    filled = jnp.zeros((*x.shape[:dim], size * span, *x.shape[dim + 1 :]), x.dtype)
+    filled = lax.dynamic_update_slice_in_dim(filled, x, index * span, axis=dim)
+    from_left = from_right = x
+    half = size // 2
+    for hop in range(1, half + 1):
+        from_left = lax.ppermute(from_left, axis, right)
+        filled = lax.dynamic_update_slice_in_dim(
+            filled, from_left, (index - hop) % size * span, axis=dim
+        )
+        if hop < size - half:
+            from_right = lax.ppermute(from_right, axis, left)
+            filled = lax.dynamic_update_slice_in_dim(
+                filled, from_right, (index + hop) % size * span, axis=dim
+            )
+    return filled
 
 
 def local(features, cotangent, w_self, w_neigh, bias, send_rows, edge_src, edge_dst, tile_count):
@@ -50,7 +71,7 @@
     scaled = (
         jnp.dot(upstream, w_neigh.T, preferred_element_type=jnp.float32) * inverse[:, None]
     ).astype(jnp.bfloat16)
-    spread = lax.all_gather(scaled, "src", axis=0, tiled=True)
+    spread = gather_around(scaled, "src", 0)
     contrib = jnp.where(active[:, None], spread[targets], zero_half).astype(jnp.float32)
     grad_table = (
         jnp.zeros((node_rows + halo_total, feature_width), jnp.float32).at[sources].add(contrib)

time: 408 us -> 373 us (0.914)
  other arithmetic: 235 us -> 211 us
  waiting for transfers between devices: 96.1 us -> 79.4 us
  local copies, waits for them, and re-layouts: 5.95 us -> 10.7 us
    all_gather x1 -> x0, waiting for transfers between devices: 31.2 us -> none  [local(): spread = lax.all_gather(scaled, 'src', axis=0, tiled=True)]
    scatter-add x1, other arithmetic: 100 us -> 76.1 us  [local(): jnp.zeros((node_rows + halo_total, feature_width), jnp.float32).at[sources]]
    ppermute x0 -> x3, waiting for transfers between devices: none -> 14.5 us  [the longest x2 14.5 us: gather_around(): from_left = lax.ppermute(from_left, axis, right)]
    ppermute x0 -> x3, starting transfers between devices: none -> 8.59 us  [the longest x1 4.57 us: gather_around(): from_right = lax.ppermute(from_right, axis, left)]
    all_to_all x1, starting transfers between devices: 16.8 us -> 11.1 us  [local(): lax.all_to_all(remote_grad.reshape(peer_total, capacity, feature_width).a...]
  transfers between devices with their start and end apart: 4 -> 6, of which waited for: 3 -> 4; matrix products, arithmetic and copies ran while one was open for 11% -> 13% of each run, Pallas kernels for 0% -> 0%
where the time goes in v1:
time: 373 us
  other arithmetic  211 us (57%)
  waiting for transfers between devices  79.4 us (21%)
  starting transfers between devices  39.2 us (11%)
  between operations  15 us (4%)
  blocking collectives  13.1 us (4%)
  local copies, waits for them, and re-layouts  10.7 us (3%)
  matrix products  4.51 us (1%)
    scatter-add x1, other arithmetic, local(): partial_value = jnp.zeros((part_total, feature_width), jnp.float32).at[ta...  76.8 us
    scatter-add x1, other arithmetic, local(): jnp.zeros((node_rows + halo_total, feature_width), jnp.float32).at[sources]  76.1 us
    scatter-add x1, other arithmetic, local(): jnp.zeros((part_total,), jnp.float32).at[targets]  43.2 us
    all_to_all x1, waiting for transfers between devices, local(): lax.all_to_all(picked, 'dom', split_axis=0, concat_axis=0, tiled=True)  32.7 us
    all_to_all x1, waiting for transfers between devices, local(): lax.all_to_all(remote_grad.reshape(peer_total, capacity, feature_width).a...  32.1 us
    all_to_all x1, starting transfers between devices, local(): lax.all_to_all(picked, 'dom', split_axis=0, concat_axis=0, tiled=True)  19.5 us
    ppermute x2, waiting for transfers between devices, gather_around(): from_left = lax.ppermute(from_left, axis, right)  14.5 us
    psum x1, blocking collectives, local(): degree_all = lax.psum(counts, 'src')  13.1 us
  transfers between devices with their start and end apart: 6, of which 4 were waited for; matrix products, arithmetic and copies ran while one was open for 13% of the time, Pallas kernels for 0%

profile of v1, /device:TPU:33, one launch (start us, length us, event | category | flops | bytes accessed | tf_op | source)
XLA Modules:
  0.0 372.7 jit_solution(11823199164143056443)
XLA Ops:
  7.2 0.7 compare_select_fusion.2
  8.9 4.6 %gather_fusion = bf16[1024,256]{1,0:T(8,128)(2,1)S(1)} fusion(bf16[1024,256]{1,0:T(8,128)(2,1)} %param.9, s32[1024]{0:T(1024)S(1)} %broadcast_clamp_fusion.2), kind=kCustom, calls=%fused_computation | custom fusion | bytes 1052672 | tf_op jit(solution)/shard_map/gather | solution.py:42
  13.5 1.0 bitcast_select_fusion
  14.5 19.5 %all-to-all-start = ((bf16[128,8,256]{2,1,0:T(8,128)(2,1)}), bf16[128,8,256]{2,1,0:T(8,128)(2,1)S(1)}, u32[]{:S(2)}, u32[]{:S(2)}) async-start(bf16[128,8,256]{2,1,0:T(8,128)(2,1)} %bitcast_select_fusion), calls=%async_computation | async-start | bytes 1048576 | tf_op jit(solution)/shard_map/all_to_all | solution.py:47
  34.9 32.7 %all-to-all-done = bf16[128,8,256]{2,1,0:T(8,128)(2,1)S(1)} async-done(((bf16[128,8,256]{2,1,0:T(8,128)(2,1)}), bf16[128,8,256]{2,1,0:T(8,128)(2,1)S(1)}, u32[]{:S(2)}, u32[]{:S(2)}) %all-to-all-start) | async-done | bytes 524320 | tf_op jit(solution)/shard_map/all_to_all | solution.py:47
  67.7 76.8 %scatter_custom_fusion = f32[4096,256]{1,0:T(8,128)} fusion(s32[8192]{0:T(1024)S(1)} %bitcast.39, pred[8192]{0:T(1024)(128)(4,1)S(1)} %fusion.19, bf16[]{:T(256)} %constant.64.clone.1, f32[]{:T(128)} %constant.57.clone.1, bf16[2048,256]{1,0:T(8,128)(2,1)S(1)} %pad_maximum_fusion, s32[8192]{0:T(1024)S(1)} %broadcast_clamp_fusion.1), kind=kCustom, calls=%fused_computation.9 | custom fusion | flops 6291456 | bytes 5283846 | tf_op jit(solution)/shard_map/scatter-add | solution.py:55
  144.5 3.7 convert_element_type.41
  148.3 43.2 %scatter_custom_fusion.1 = f32[4096]{0:T(1024)S(1)} fusion(s32[8192]{0:T(1024)S(1)} %bitcast.40, f32[8192]{0:T(1024)S(1)} %fusion.25, f32[]{:T(128)} %constant.57.clone.1), kind=kCustom, calls=%fused_computation.50 | custom fusion | flops 8192 | bytes 16388 | tf_op jit(solution)/shard_map/scatter-add | solution.py:43
  191.5 13.1 %psum.7 = f32[4096]{0:T(1024)S(1)} all-reduce(f32[4096]{0:T(1024)S(1)} %scatter_custom_fusion.1), channel_id=1, replica_groups=mesh['dom'=128,'src'=4] {'src'}, use_global_device_ids=true, to_apply=%region_3.4 | all-reduce | flops 4096 | bytes 32768 | tf_op jit(solution)/shard_map/psum | solution.py:44
  205.0 2.6 multiply_convert_fusion
  208.1 1.9 collective-permute-start
  210.0 4.6 %collective-permute-start.1 = (bf16[1024,256]{1,0:T(8,128)(2,1)S(1)}, bf16[1024,256]{1,0:T(8,128)(2,1)}, u32[]{:S(2)}, u32[]{:S(2)}) collective-permute-start(bf16[1024,256]{1,0:T(8,128)(2,1)S(1)} %get-tuple-element.7), channel_id=1, source_target_pairs={{0,3},{1,0},{2,1},{3,2},{4,7},{5,4},{6,5},{7,6},{8,11},{9,8},{10,9... | collective-permute-start | bytes 1572872 | tf_op jit(solution)/shard_map/ppermute | solution.py:21
  214.6 6.5 %collective-permute-done = bf16[1024,256]{1,0:T(8,128)(2,1)} collective-permute-done((bf16[1024,256]{1,0:T(8,128)(2,1)S(1)}, bf16[1024,256]{1,0:T(8,128)(2,1)}, u32[]{:S(2)}, u32[]{:S(2)}) %collective-permute-start) | collective-permute-done | bytes 524320 | tf_op jit(solution)/shard_map/ppermute | solution.py:16
  221.1 2.1 collective-permute-start.2
  223.3 1.1 constant_dynamic-update-slice_fusion.2
  224.4 1.1 constant_dynamic-update-slice_fusion.1
  225.5 8.0 %collective-permute-done.2 = bf16[1024,256]{1,0:T(8,128)(2,1)} collective-permute-done((bf16[1024,256]{1,0:T(8,128)(2,1)}, bf16[1024,256]{1,0:T(8,128)(2,1)}, u32[]{:S(2)}, u32[]{:S(2)}) %collective-permute-start.2) | collective-permute-done | bytes 524320 | tf_op jit(solution)/shard_map/ppermute | solution.py:16
  233.5 1.1 constant_dynamic-update-slice_fusion
  234.5 76.1 %scatter_custom_fusion.2 = f32[2048,256]{1,0:T(8,128)} fusion(s32[8192]{0:T(1024)S(1)} %bitcast.38, pred[8192]{0:T(1024)(128)(4,1)S(1)} %fusion.19, bf16[]{:T(256)} %constant.64.clone.1, f32[]{:T(128)} %constant.57.clone.1, bf16[4096,256]{1,0:T(8,128)(2,1)S(1)} %constant_dynamic-update-slice_fusion, s32[8192]{0:T(1024)S(1)} %broadcast_clamp_fusion), kind=kCustom, calls=%fused_computation.7 | custom fusion | flops 6291456 | bytes 4235270 | tf_op jit(solution)/shard_map/scatter-add | solution.py:77
  310.6 2.2 fusion.16
  312.9 11.1 %all-to-all-start.1 = ((bf16[128,8,256]{2,1,0:T(8,128)(2,1)}), bf16[128,8,256]{2,1,0:T(8,128)(2,1)S(1)}, u32[]{:S(2)}, u32[]{:S(2)}) async-start(bf16[128,8,256]{2,1,0:T(8,128)(2,1)} %fusion.16), calls=%async_computation.2 | async-start | bytes 1048576 | tf_op jit(solution)/shard_map/all_to_all | solution.py:81
  324.2 1.3 slice_add_fusion
  325.5 32.1 %all-to-all-done.1 = bf16[128,8,256]{2,1,0:T(8,128)(2,1)S(1)} async-done(((bf16[128,8,256]{2,1,0:T(8,128)(2,1)}), bf16[128,8,256]{2,1,0:T(8,128)(2,1)S(1)}, u32[]{:S(2)}, u32[]{:S(2)}) %all-to-all-start.1) | async-done | bytes 524320 | tf_op jit(solution)/shard_map/all_to_all | solution.py:81
  357.6 8.3 %scatter_custom_fusion.3 = f32[1024,256]{1,0:T(8,128)} fusion(f32[1024,256]{1,0:T(8,128)} %slice_add_fusion, s32[1024]{0:T(1024)S(1)} %reshape.175, bf16[128,8,256]{2,1,0:T(8,128)(2,1)S(1)} %all-to-all-done.1), kind=kCustom, calls=%fused_computation.25 | custom fusion | flops 524288 | bytes 1572864 | tf_op jit(solution)/shard_map/scatter-add | solution.py:90
  (39 shorter events, 2.3 us)
Async XLA Ops:
  7.2 197.9 %copy-start = (bf16[256,256]{1,0:T(8,128)(2,1)S(1)}, bf16[256,256]{1,0:T(8,128)(2,1)}, u32[]{:S(2)}) copy-start(bf16[256,256]{1,0:T(8,128)(2,1)} %param.12) | copy-start | bytes 393220
  13.5 21.2 %copy-start.4 = (s32[1,1,8192]{2,1,0:T(1,128)S(1)}, s32[1,1,8192]{2,1,0:T(1,128)}, u32[]{:S(2)}) copy-start(s32[1,1,8192]{2,1,0:T(1,128)} %param.15) | copy-start | bytes 98308
  13.5 21.3 %copy-start.5 = (s32[1,1,8192]{2,1,0:T(1,128)S(1)}, s32[1,1,8192]{2,1,0:T(1,128)}, u32[]{:S(2)}) copy-start(s32[1,1,8192]{2,1,0:T(1,128)} %param.16) | copy-start | bytes 98308
  13.5 54.1 %copy-start.1 = (bf16[1024,256]{1,0:T(8,128)(2,1)S(1)}, bf16[1024,256]{1,0:T(8,128)(2,1)}, u32[]{:S(2)}) copy-start(bf16[1024,256]{1,0:T(8,128)(2,1)} %param.9) | copy-start | bytes 1572868
  14.5 53.1 %all-to-all-start = ((bf16[128,8,256]{2,1,0:T(8,128)(2,1)}), bf16[128,8,256]{2,1,0:T(8,128)(2,1)S(1)}, u32[]{:S(2)}, u32[]{:S(2)}) async-start(bf16[128,8,256]{2,1,0:T(8,128)(2,1)} %bitcast_select_fusion), calls=%async_computation | async-start | bytes 1048576 | tf_op jit(solution)/shard_map/all_to_all | solution.py:47
  34.0 171.0 %reduce-scatter.2.cloned.1.call-start = ((), (), s32[]{:S(2)}) async-start(), calls=%async_computation.3 | async-start | bytes 2621440 | tf_op jit(solution)/shard_map/reduce_scatter | solution.py:57
  148.2 43.3 %copy-start.7 = (bf16[256]{0:T(256)(128)(2,1)S(1)}, bf16[256]{0:T(256)(128)(2,1)}, u32[]{:S(2)}) copy-start(bf16[256]{0:T(256)(128)(2,1)} %param.13) | copy-start | bytes 1540
  148.2 56.4 %copy-start.3 = (bf16[256,256]{1,0:T(8,128)(2,1)S(1)}, bf16[256,256]{1,0:T(8,128)(2,1)}, u32[]{:S(2)}) copy-start(bf16[256,256]{1,0:T(8,128)(2,1)} %param.11) | copy-start | bytes 393220
  148.3 56.8 %copy-start.6 = (bf16[1024,256]{1,0:T(8,128)(2,1)S(1)}, bf16[1024,256]{1,0:T(8,128)(2,1)}, u32[]{:S(2)}) copy-start(bf16[1024,256]{1,0:T(8,128)(2,1)} %param.10) | copy-start | bytes 1572868
  208.1 13.0 %collective-permute-start = (bf16[1024,256]{1,0:T(8,128)(2,1)S(1)}, bf16[1024,256]{1,0:T(8,128)(2,1)}, u32[]{:S(2)}, u32[]{:S(2)}) collective-permute-start(bf16[1024,256]{1,0:T(8,128)(2,1)S(1)} %get-tuple-element.7), channel_id=1, source_target_pairs={{0,1},{1,2},{2,3},{3,0},{4,5},{5,6},{6,7},{7,4},{8,9},{9,10},{10,1... | collective-permute-start | bytes 1572872 | tf_op jit(solution)/shard_map/ppermute | solution.py:16
  210.0 14.4 %collective-permute-start.1 = (bf16[1024,256]{1,0:T(8,128)(2,1)S(1)}, bf16[1024,256]{1,0:T(8,128)(2,1)}, u32[]{:S(2)}, u32[]{:S(2)}) collective-permute-start(bf16[1024,256]{1,0:T(8,128)(2,1)S(1)} %get-tuple-element.7), channel_id=1, source_target_pairs={{0,3},{1,0},{2,1},{3,2},{4,7},{5,4},{6,5},{7,6},{8,11},{9,8},{10,9... | collective-permute-start | bytes 1572872 | tf_op jit(solution)/shard_map/ppermute | solution.py:21
  221.1 12.3 %collective-permute-start.2 = (bf16[1024,256]{1,0:T(8,128)(2,1)}, bf16[1024,256]{1,0:T(8,128)(2,1)}, u32[]{:S(2)}, u32[]{:S(2)}) collective-permute-start(bf16[1024,256]{1,0:T(8,128)(2,1)} %collective-permute-done), channel_id=1, source_target_pairs={{0,1},{1,2},{2,3},{3,0},{4,5},{5,6},{6,7},{7,4},{8,9},{9,10},{10,1... | collective-permute-start | bytes 1572872 | tf_op jit(solution)/shard_map/ppermute | solution.py:16
  310.6 13.5 %copy-start.2 = (f32[2048,256]{1,0:T(8,128)S(1)}, f32[2048,256]{1,0:T(8,128)}, u32[]{:S(2)}) copy-start(f32[2048,256]{1,0:T(8,128)} %scatter_custom_fusion.2) | copy-start | bytes 6291460
  312.9 44.7 %all-to-all-start.1 = ((bf16[128,8,256]{2,1,0:T(8,128)(2,1)}), bf16[128,8,256]{2,1,0:T(8,128)(2,1)S(1)}, u32[]{:S(2)}, u32[]{:S(2)}) async-start(bf16[128,8,256]{2,1,0:T(8,128)(2,1)} %fusion.16), calls=%async_computation.2 | async-start | bytes 1048576 | tf_op jit(solution)/shard_map/all_to_all | solution.py:81
Sparse Core Ops, SparseCore 0:
  148.4 28.3 reduce-scatter.1
